TPU v7x, 32 devices: a whole 2x2x4 slice. The times are simulated.
32 devices in a mesh: groups: 2 (over x), row: 8 (over z, y), col: 2 (over core).
Axes of the slice: x: 2, y: 2, z: 4, core: 2. Of those that a mesh axis runs over, the one named last changes fastest.
Arguments:
- start_field: float32 [1024, 384, 256], P(('groups', 'row'), 'col'), parts along dimension 0, may hold values from 0 to 2
- counts: int32 [1024, 384, 256], P('groups', 'row', 'col'), parts along dimension 0, may hold values from -40 to 40
- weights: int32 [1024, 384, 256], P('groups', 'row', 'col'), parts along dimension 0, may hold values from 1 to 16
- strat_one: int32 [512, 512], replicated, may hold values from -64 to 63
- strat_two: int32 [384, 384], replicated, may hold values from -64 to 63
- strat_three: int32 [256, 256], replicated, may hold values from -64 to 63
Outputs:
- estimate: float32 [1024, 384, 256], P(('groups', 'row'), 'col'), parts along dimension 0
There are 2 independent parts, one for each index of `groups`. A program takes and returns all parts, laid end to end along the dimension named above; an argument that names none is the same for every part. Nothing has to cross between parts.
All inputs are finite; a program needn't handle non-finite values.
Results may differ from a plain program's by a relative error of at most 0.0001.
Values sent between devices are 32-bit elements; how exact they have to be, the bound alone decides.
No kernel may reach another device: no remote copies, remote signals or barrier semaphores. Data moves between devices by JAX's collectives and lax.ppermute only.
A program may use at most 128 MiB of HBM per device.

v0:
```python
import math
import jax
import jax.numpy as jnp
from jax import lax
from jax.sharding import PartitionSpec as P

highest = lax.Precision.HIGHEST
step_size = 0.5


def scaled(quant):
    order = quant.shape[0]
    return quant.astype(jnp.float32) * (1.0 / (37.0 * math.sqrt(order)))


def along_first(matrix, field):
    return jnp.einsum("ji,iab->jab", matrix, field, precision=highest)


def along_second(matrix, field):
    return jnp.einsum("ji,aib->ajb", matrix, field, precision=highest)


def along_third(matrix, field):
    return jnp.einsum("ji,abi->abj", matrix, field, precision=highest)


def pencil_forward(field, first, second, third):
    field = along_third(third, field)
    field = along_second(
        second, lax.all_to_all(field, "col", split_axis=2, concat_axis=1, tiled=True)
    )
    return along_first(first, lax.all_to_all(field, "row", split_axis=1, concat_axis=0, tiled=True))


def pencil_adjoint(field, first, second, third):
    field = along_first(first.T, field)
    field = along_second(
        second.T, lax.all_to_all(field, "row", split_axis=0, concat_axis=1, tiled=True)
    )
    return along_third(
        third.T, lax.all_to_all(field, "col", split_axis=1, concat_axis=2, tiled=True)
    )


def per_device(start_field, counts, weights, strat_one, strat_two, strat_three):
    first = scaled(strat_one)
    second = scaled(strat_two)
    third = scaled(strat_three)
    weight_field = weights.astype(jnp.float32) / 16.0
    target = counts.astype(jnp.float32) / 16.0
    estimate = start_field
    image = pencil_forward(estimate, first, second, third)
    residual = weight_field * (image - target)
    gradient = pencil_adjoint(residual, first, second, third)
    estimate = jnp.maximum(estimate - step_size * gradient, 0.0)
    return estimate


def solution(mesh):
    placed = (
        P(("groups", "row"), "col", None),
        P("groups", "row", "col"),
        P("groups", "row", "col"),
        P(),
        P(),
        P(),
    )
    return jax.shard_map(
        per_device,
        mesh=mesh,
        in_specs=placed,
        out_specs=P(("groups", "row"), "col", None),
        check_vma=False,
    )
```

profile of v0, /device:TPU:0, one launch (start us, length us, event | category | flops | bytes accessed | tf_op | source)
XLA Modules:
  0.0 937.4 jit_solution(8232785942097816457)
XLA Ops:
  0.0 14.9 %convolution_bitcast_fusion.2 = f32[64,192,256]{2,1,0:T(8,128)} fusion(f32[64,192,256]{2,1,0:T(8,128)} %param.6, s32[256,256]{1,0:T(8,128)} %param.11), kind=kOutput, calls=%fused_computation.13 | convolution fusion | flops 9663807488 | bytes 25427968 | tf_op jit(solution)/shard_map/ji,abi->abj/dot_general | solution.py:25
  14.9 17.4 %copy.37 = f32[64,192,256]{1,0,2:T(8,128)} copy(f32[64,192,256]{2,1,0:T(8,128)} %convolution_bitcast_fusion.2) | data formatting | bytes 25165824 | tf_op jit(solution)/shard_map/ji,abi->abj/dot_general | solution.py:25
  32.3 31.8 %all_to_all.72 = f32[64,192,256]{1,0,2:T(8,128)} all-to-all(f32[64,192,256]{1,0,2:T(8,128)} %copy.37), channel_id=1, replica_groups=mesh['groups'=2,'row'=8,'col'=2] {'col'}, dimensions={2} | all-to-all | bytes 25165824 | tf_op jit(solution)/shard_map/all_to_all | solution.py:31
  64.1 17.9 %copy.57 = f32[64,192,2,128]{3,2,1,0:T(2,128)} copy(f32[64,192,2,128]{1,0,3,2:T(8,128)} %bitcast.42) | data formatting | bytes 25165824 | tf_op jit(solution)/shard_map/all_to_all | solution.py:31
  82.1 0.0 copy-start.1
  82.1 11.0 %copy.39 = f32[64,2,192,128]{3,2,1,0:T(8,128)} copy(f32[64,2,192,128]{3,1,2,0:T(2,128)} %bitcast.44) | data formatting | bytes 25165824 | tf_op jit(solution)/shard_map/all_to_all | solution.py:31
  93.0 0.0 copy-done.1
  93.0 43.6 %convolution_bitcast_fusion.1 = f32[64,384,128]{1,2,0:T(8,128)} fusion(f32[64,384,128]{2,1,0:T(8,128)} %bitcast.40, s32[384,384]{1,0:T(8,128)S(1)} %copy-done.1), kind=kOutput, calls=%fused_computation.12 | convolution fusion | flops 14495809536 | bytes 25755648 | tf_op jit(solution)/shard_map/ji,aib->ajb/dot_general | solution.py:21
  136.6 12.7 %copy.41 = f32[64,384,128]{2,0,1:T(8,128)} copy(f32[64,384,128]{1,2,0:T(8,128)} %convolution_bitcast_fusion.1) | data formatting | bytes 25165824 | tf_op jit(solution)/shard_map/ji,aib->ajb/transpose | solution.py:21
  149.4 281.8 %all_to_all.73 = f32[64,384,128]{2,0,1:T(8,128)} all-to-all(f32[64,384,128]{2,0,1:T(8,128)} %copy.41), channel_id=1, replica_groups=mesh['groups'=2,'row'=8,'col'=2] {'row'}, dimensions={1} | all-to-all | bytes 25165824 | tf_op jit(solution)/shard_map/all_to_all | solution.py:33
  431.2 0.0 copy-start
  431.2 16.5 %copy.43 = f32[8,64,48,128]{3,2,1,0:T(8,128)} copy(f32[8,64,48,128]{3,1,2,0:T(8,128)} %bitcast.45) | data formatting | bytes 25165824 | tf_op jit(solution)/shard_map/all_to_all | solution.py:33
  447.7 0.0 copy-done
  447.7 28.6 %fusion.5 = f32[512,48,128]{2,0,1:T(8,128)S(1)} fusion(f32[512,48,128]{2,1,0:T(8,128)} %bitcast.43, s32[512,512]{1,0:T(8,128)S(1)} %copy-done), kind=kOutput, calls=%fused_computation.5 | convolution fusion | flops 19327877120 | bytes 26214400 | tf_op jit(solution)/shard_map/ji,iab->jab/dot_general | solution.py:17
  476.4 38.4 %fusion.3 = f32[512,48,128]{2,0,1:T(8,128)} fusion(f32[512,48,128]{2,0,1:T(8,128)S(1)} %fusion.5, s32[512,48,128]{2,1,0:T(8,128)} %param.7, s32[512,48,128]{2,1,0:T(8,128)} %param.8, s32[512,512]{1,0:T(8,128)S(1)} %copy-done), kind=kOutput, calls=%fused_computation.4 | convolution fusion | flops 19346751488 | bytes 51380224 | tf_op jit(solution)/shard_map/ji,iab->jab/dot_general | solution.py:17
  514.8 16.4 %copy.47 = f32[512,48,128]{2,1,0:T(8,128)} copy(f32[512,48,128]{2,0,1:T(8,128)} %fusion.3) | data formatting | bytes 25165824 | tf_op jit(solution)/shard_map/ji,iab->jab/dot_general | solution.py:17
  531.2 279.9 %all_to_all.74 = f32[512,48,128]{2,1,0:T(8,128)} all-to-all(f32[512,48,128]{2,1,0:T(8,128)} %copy.47), channel_id=1, replica_groups=mesh['groups'=2,'row'=8,'col'=2] {'row'}, dimensions={0} | all-to-all | bytes 25165824 | tf_op jit(solution)/shard_map/all_to_all | solution.py:39
  811.1 11.2 %copy.48 = f32[64,8,48,128]{3,2,1,0:T(8,128)} copy(f32[64,8,48,128]{3,2,0,1:T(8,128)} %bitcast.46) | data formatting | bytes 25165824 | tf_op jit(solution)/shard_map/all_to_all | solution.py:39
  822.3 27.5 %convolution_bitcast_fusion = f32[64,384,128]{1,2,0:T(8,128)} fusion(f32[64,384,128]{2,1,0:T(8,128)} %bitcast.41, s32[384,384]{1,0:T(8,128)S(1)} %copy-done.1), kind=kOutput, calls=%fused_computation.11 | convolution fusion | flops 14495809536 | bytes 25755648 | tf_op jit(solution)/shard_map/ji,aib->ajb/dot_general | solution.py:21
  849.8 12.6 %copy.50 = f32[64,384,128]{2,0,1:T(8,128)} copy(f32[64,384,128]{1,2,0:T(8,128)} %convolution_bitcast_fusion) | data formatting | bytes 25165824 | tf_op jit(solution)/shard_map/ji,aib->ajb/transpose | solution.py:21
  862.4 15.9 %all_to_all.75 = f32[64,384,128]{2,0,1:T(8,128)S(1)} all-to-all(f32[64,384,128]{2,0,1:T(8,128)} %copy.50), channel_id=1, replica_groups=mesh['groups'=2,'row'=8,'col'=2] {'col'}, dimensions={1} | all-to-all | bytes 25165824 | tf_op jit(solution)/shard_map/all_to_all | solution.py:42
  878.3 23.4 %copy.52 = f32[64,192,2,128]{3,2,1,0:T(2,128)} copy(f32[64,192,2,128]{3,0,1,2:T(8,128)S(1)} %bitcast.47) | data formatting | bytes 25165824 | tf_op jit(solution)/shard_map/all_to_all | solution.py:42
  901.7 0.0 copy-start.2
  901.7 16.6 %all_to_all.67 = f32[64,192,256]{2,1,0:T(8,128)} reshape(f32[64,192,2,128]{3,2,1,0:T(2,128)} %copy.52) | data formatting | bytes 25165824 | tf_op jit(solution)/shard_map/all_to_all | solution.py:42
  918.3 0.0 copy-done.2
  918.3 18.6 %subtract_maximum_fusion = f32[64,192,256]{2,1,0:T(8,128)} fusion(f32[64,192,256]{2,1,0:T(8,128)} %param.6, f32[64,192,256]{2,1,0:T(8,128)} %all_to_all.67, s32[256,256]{1,0:T(8,128)S(1)} %copy-done.2), kind=kOutput, calls=%fused_computation.9 | convolution fusion | flops 9673244672 | bytes 38010880 | tf_op jit(solution)/shard_map/ji,abi->abj/dot_general | solution.py:25
Async XLA Ops:
  82.1 11.0 %copy-start.1 = (s32[384,384]{1,0:T(8,128)S(1)}, s32[384,384]{1,0:T(8,128)}, u32[]{:S(2)}) copy-start(s32[384,384]{1,0:T(8,128)} %param.10) | copy-start | bytes 1769476
  431.2 16.5 %copy-start = (s32[512,512]{1,0:T(8,128)S(1)}, s32[512,512]{1,0:T(8,128)}, u32[]{:S(2)}) copy-start(s32[512,512]{1,0:T(8,128)} %param.9) | copy-start | bytes 3145732
  901.7 16.6 %copy-start.2 = (s32[256,256]{1,0:T(8,128)S(1)}, s32[256,256]{1,0:T(8,128)}, u32[]{:S(2)}) copy-start(s32[256,256]{1,0:T(8,128)} %param.11) | copy-start | bytes 786436
where the time goes:
time: 943 us; the launch traced here: 937 us
  blocking collectives  609 us (65%)
  matrix products  172 us (18%)
  local copies, waits for them, and re-layouts  156 us (17%)
    all_to_all x1, blocking collectives, pencil_forward(): lax.all_to_all(field, 'row', split_axis=1, concat_axis=0, tiled=True)  282 us
    all_to_all x1, blocking collectives, pencil_adjoint(): lax.all_to_all(field, 'row', split_axis=0, concat_axis=1, tiled=True)  280 us
    dot_general x2, matrix products, along_second(): return jnp.einsum('ji,aib->ajb', matrix, field, precision=highest)  71.1 us
    dot_general x2, matrix products, along_first(): return jnp.einsum('ji,iab->jab', matrix, field, precision=highest)  67 us
    all_to_all x2, local copies, waits for them, and re-layouts, pencil_adjoint(): lax.all_to_all(field, 'col', split_axis=1, concat_axis=2, tiled=True)  39.9 us
    dot_general x2, matrix products, along_third(): return jnp.einsum('ji,abi->abj', matrix, field, precision=highest)  33.5 us
    all_to_all x1, blocking collectives, pencil_forward(): lax.all_to_all(field, 'col', split_axis=2, concat_axis=1, tiled=True)  31.8 us
    all_to_all x2, local copies, waits for them, and re-layouts, pencil_forward(): lax.all_to_all(field, 'col', split_axis=2, concat_axis=1, tiled=True)  28.9 us

commit v1 on v0

--- a/solution.py
+++ b/solution.py
@@ -30,7 +30,13 @@
     field = along_second(
         second, lax.all_to_all(field, "col", split_axis=2, concat_axis=1, tiled=True)
     )
-    return along_first(first, lax.all_to_all(field, "row", split_axis=1, concat_axis=0, tiled=True))
+    return along_first(
+        first,
+        jnp.concatenate(
+            lax.all_to_all(jnp.stack(jnp.split(field, lax.axis_size("row"), axis=1)), "row", 0, 0),
+            axis=0,
+        ),
+    )
 
 
 def pencil_adjoint(field, first, second, third):

time: 943 us -> 984 us (1.043)
  local copies, waits for them, and re-layouts: 156 us -> 203 us
    another operation x0 -> x10, local copies, waits for them, and re-layouts: none -> 56.1 us  [pencil_forward(): jnp.stack(jnp.split(field, lax.axis_size('row'), axis=1))]
    transpose x2 -> x1, local copies, waits for them, and re-layouts: 25.4 us -> 12.6 us  [along_second(): return jnp.einsum('ji,aib->ajb', matrix, field, precision=highest)]
where the time goes in v1:
time: 984 us; the launch traced here: 978 us
  blocking collectives  608 us (62%)
  local copies, waits for them, and re-layouts  203 us (21%)
  matrix products  167 us (17%)
    all_to_all x1, blocking collectives, pencil_forward(): lax.all_to_all(jnp.stack(jnp.split(field, lax.axis_size('row'), axis=1)),...  281 us
    all_to_all x1, blocking collectives, pencil_adjoint(): lax.all_to_all(field, 'row', split_axis=0, concat_axis=1, tiled=True)  280 us
    dot_general x2, matrix products, along_second(): return jnp.einsum('ji,aib->ajb', matrix, field, precision=highest)  71.1 us
    dot_general x2, matrix products, along_first(): return jnp.einsum('ji,iab->jab', matrix, field, precision=highest)  62 us
    another operation x10, local copies, waits for them, and re-layouts, pencil_forward(): jnp.stack(jnp.split(field, lax.axis_size('row'), axis=1))  56.1 us
    all_to_all x2, local copies, waits for them, and re-layouts, pencil_adjoint(): lax.all_to_all(field, 'col', split_axis=1, concat_axis=2, tiled=True)  40 us
    dot_general x2, matrix products, along_third(): return jnp.einsum('ji,abi->abj', matrix, field, precision=highest)  33.5 us
    all_to_all x1, blocking collectives, pencil_forward(): lax.all_to_all(field, 'col', split_axis=2, concat_axis=1, tiled=True)  31.8 us

profile of v1, /device:TPU:0, one launch (start us, length us, event | category | flops | bytes accessed | tf_op | source)
XLA Modules:
  0.0 978.2 jit_solution(9219939643596086590)
XLA Ops:
  0.0 14.9 %convolution_bitcast_fusion.2 = f32[64,192,256]{2,1,0:T(8,128)} fusion(f32[64,192,256]{2,1,0:T(8,128)} %param.6, s32[256,256]{1,0:T(8,128)} %param.11), kind=kOutput, calls=%fused_computation.11 | convolution fusion | flops 9663807488 | bytes 25427968 | tf_op jit(solution)/shard_map/ji,abi->abj/dot_general | solution.py:25
  14.9 17.4 %copy.40 = f32[64,192,256]{1,0,2:T(8,128)} copy(f32[64,192,256]{2,1,0:T(8,128)} %convolution_bitcast_fusion.2) | data formatting | bytes 25165824 | tf_op jit(solution)/shard_map/ji,abi->abj/dot_general | solution.py:25
  32.3 31.8 %all_to_all.59 = f32[64,192,256]{1,0,2:T(8,128)} all-to-all(f32[64,192,256]{1,0,2:T(8,128)} %copy.40), channel_id=1, replica_groups=mesh['groups'=2,'row'=8,'col'=2] {'col'}, dimensions={2} | all-to-all | bytes 25165824 | tf_op jit(solution)/shard_map/all_to_all | solution.py:31
  64.2 17.9 %copy.65 = f32[64,192,2,128]{3,2,1,0:T(2,128)} copy(f32[64,192,2,128]{1,0,3,2:T(8,128)} %bitcast.56) | data formatting | bytes 25165824 | tf_op jit(solution)/shard_map/all_to_all | solution.py:31
  82.1 0.0 copy-start.3
  82.1 10.9 %copy.42 = f32[64,2,192,128]{3,2,1,0:T(8,128)} copy(f32[64,2,192,128]{3,1,2,0:T(2,128)} %bitcast.58) | data formatting | bytes 25165824 | tf_op jit(solution)/shard_map/all_to_all | solution.py:31
  93.0 0.0 copy-done.3
  93.0 43.6 %convolution_bitcast_fusion.1 = f32[64,384,128]{1,2,0:T(8,128)} fusion(f32[64,384,128]{2,1,0:T(8,128)} %bitcast.54, s32[384,384]{1,0:T(8,128)S(1)} %copy-done.3), kind=kOutput, calls=%fused_computation.10 | convolution fusion | flops 14495809536 | bytes 25755648 | tf_op jit(solution)/shard_map/ji,aib->ajb/dot_general | solution.py:21
  136.6 28.2 %slice_bitcast_fusion = (f32[1,64,48,128]{2,3,1,0:T(8,128)}, f32[1,64,48,128]{2,3,1,0:T(8,128)}, f32[1,64,48,128]{2,3,1,0:T(8,128)}, f32[1,64,48,128]{2,3,1,0:T(...) fusion(f32[64,384,128]{1,2,0:T(8,128)} %convolution_bitcast_fus, ...), kind=kLoop, calls=%fused_computation.12 | loop fusion | bytes 25165824 | tf_op jit(solution)/shard_map/stack | solution.py:36
  164.9 2.8 copy.51
  167.7 2.8 copy.50
  170.5 3.7 copy.49
  174.2 3.7 copy.48
  177.9 3.7 copy.47
  181.6 3.7 copy.46
  185.3 3.7 copy.45
  189.0 3.7 copy.44
  192.7 0.0 copy-start.1
  192.7 0.0 copy-start
  192.7 1.7 constant_dynamic-update-slice_fusion.7
  194.4 1.5 constant_dynamic-update-slice_fusion.6
  195.9 1.5 constant_dynamic-update-slice_fusion.5
  197.4 1.5 constant_dynamic-update-slice_fusion.4
  198.9 0.0 copy-done.1
  198.9 0.1 constant_dynamic-update-slice_fusion.3
  199.0 0.0 copy-done
  199.0 0.1 constant_dynamic-update-slice_fusion.2
  199.2 0.1 constant_dynamic-update-slice_fusion.1
  199.3 0.1 constant_dynamic-update-slice_fusion
  199.4 280.8 %all_to_all.60 = f32[8,64,48,128]{3,2,1,0:T(8,128)} all-to-all(f32[8,64,48,128]{3,2,1,0:T(8,128)S(1)} %constant_dynamic-update-slice_fusion), channel_id=1, replica_groups=mesh['groups'=2,'row'=8,'col'=2] {'row'}, dimensions={0} | all-to-all | bytes 25165824 | tf_op jit(solution)/shard_map/all_to_all | solution.py:36
  480.2 0.0 copy-start.2
  480.2 13.5 %copy.52 = f32[8,64,48,128]{3,1,0,2:T(8,128)} copy(f32[8,64,48,128]{3,2,1,0:T(8,128)} %all_to_all.60) | data formatting | bytes 25165824 | tf_op jit(solution)/shard_map/all_to_all | solution.py:36
  493.6 0.0 copy-done.2
  493.6 23.6 %fusion.8 = f32[512,48,128]{2,0,1:T(8,128)S(1)} fusion(f32[512,48,128]{2,0,1:T(8,128)} %bitcast.57, s32[512,512]{1,0:T(8,128)S(1)} %copy-done.2), kind=kOutput, calls=%fused_computation.20 | convolution fusion | flops 19327877120 | bytes 26214400 | tf_op jit(solution)/shard_map/ji,iab->jab/dot_general | solution.py:17
  517.2 38.5 %fusion.3 = f32[512,48,128]{2,0,1:T(8,128)} fusion(f32[512,48,128]{2,0,1:T(8,128)S(1)} %fusion.8, s32[512,48,128]{2,1,0:T(8,128)} %param.7, s32[512,48,128]{2,1,0:T(8,128)} %param.8, s32[512,512]{1,0:T(8,128)S(1)} %copy-done.2), kind=kOutput, calls=%fused_computation.4 | convolution fusion | flops 19346751488 | bytes 51380224 | tf_op jit(solution)/shard_map/ji,iab->jab/dot_general | solution.py:17
  555.7 16.4 %copy.55 = f32[512,48,128]{2,1,0:T(8,128)} copy(f32[512,48,128]{2,0,1:T(8,128)} %fusion.3) | data formatting | bytes 25165824 | tf_op jit(solution)/shard_map/ji,iab->jab/dot_general | solution.py:17
  572.1 279.7 %all_to_all.61 = f32[512,48,128]{2,1,0:T(8,128)} all-to-all(f32[512,48,128]{2,1,0:T(8,128)} %copy.55), channel_id=1, replica_groups=mesh['groups'=2,'row'=8,'col'=2] {'row'}, dimensions={0} | all-to-all | bytes 25165824 | tf_op jit(solution)/shard_map/all_to_all | solution.py:45
  851.8 0.0 copy-start.4
  851.8 11.3 %copy.56 = f32[64,8,48,128]{3,2,1,0:T(8,128)} copy(f32[64,8,48,128]{3,2,0,1:T(8,128)} %bitcast.59) | data formatting | bytes 25165824 | tf_op jit(solution)/shard_map/all_to_all | solution.py:45
  863.0 0.0 copy-done.4
  863.0 27.5 %convolution_bitcast_fusion = f32[64,384,128]{1,2,0:T(8,128)} fusion(f32[64,384,128]{2,1,0:T(8,128)} %bitcast.55, s32[384,384]{1,0:T(8,128)S(1)} %copy-done.4), kind=kOutput, calls=%fused_computation.9 | convolution fusion | flops 14495809536 | bytes 25755648 | tf_op jit(solution)/shard_map/ji,aib->ajb/dot_general | solution.py:21
  890.5 12.6 %copy.58 = f32[64,384,128]{2,0,1:T(8,128)} copy(f32[64,384,128]{1,2,0:T(8,128)} %convolution_bitcast_fusion) | data formatting | bytes 25165824 | tf_op jit(solution)/shard_map/ji,aib->ajb/transpose | solution.py:21
  903.1 15.9 %all_to_all.62 = f32[64,384,128]{2,0,1:T(8,128)S(1)} all-to-all(f32[64,384,128]{2,0,1:T(8,128)} %copy.58), channel_id=1, replica_groups=mesh['groups'=2,'row'=8,'col'=2] {'col'}, dimensions={1} | all-to-all | bytes 25165824 | tf_op jit(solution)/shard_map/all_to_all | solution.py:48
  919.1 23.4 %copy.60 = f32[64,192,2,128]{3,2,1,0:T(2,128)} copy(f32[64,192,2,128]{3,0,1,2:T(8,128)S(1)} %bitcast.60) | data formatting | bytes 25165824 | tf_op jit(solution)/shard_map/all_to_all | solution.py:48
  942.4 0.0 copy-start.5
  942.4 16.6 %all_to_all.54 = f32[64,192,256]{2,1,0:T(8,128)} reshape(f32[64,192,2,128]{3,2,1,0:T(2,128)} %copy.60) | data formatting | bytes 25165824 | tf_op jit(solution)/shard_map/all_to_all | solution.py:48
  959.0 0.0 copy-done.5
  959.0 18.6 %subtract_maximum_fusion = f32[64,192,256]{2,1,0:T(8,128)} fusion(f32[64,192,256]{2,1,0:T(8,128)} %param.6, f32[64,192,256]{2,1,0:T(8,128)} %all_to_all.54, s32[256,256]{1,0:T(8,128)S(1)} %copy-done.5), kind=kOutput, calls=%fused_computation.7 | convolution fusion | flops 9673244672 | bytes 38010880 | tf_op jit(solution)/shard_map/ji,abi->abj/dot_general | solution.py:25
Async XLA Ops:
  82.1 10.9 %copy-start.3 = (s32[384,384]{1,0:T(8,128)S(1)}, s32[384,384]{1,0:T(8,128)}, u32[]{:S(2)}) copy-start(s32[384,384]{1,0:T(8,128)} %param.10) | copy-start | bytes 1769476
  192.7 6.2 copy-start.1
  192.7 6.3 copy-start
  480.2 13.5 %copy-start.2 = (s32[512,512]{1,0:T(8,128)S(1)}, s32[512,512]{1,0:T(8,128)}, u32[]{:S(2)}) copy-start(s32[512,512]{1,0:T(8,128)} %param.9) | copy-start | bytes 3145732
  851.8 11.3 %copy-start.4 = (s32[384,384]{1,0:T(8,128)S(1)}, s32[384,384]{1,0:T(8,128)}, u32[]{:S(2)}) copy-start(s32[384,384]{1,0:T(8,128)} %param.10) | copy-start | bytes 1769476
  942.4 16.6 %copy-start.5 = (s32[256,256]{1,0:T(8,128)S(1)}, s32[256,256]{1,0:T(8,128)}, u32[]{:S(2)}) copy-start(s32[256,256]{1,0:T(8,128)} %param.11) | copy-start | bytes 786436
